TPU v7x, 256 devices: a whole 4x4x8 slice. The times are simulated.
256 devices in a mesh: tm: 16 (over y_lo, z), orb: 16 (over y_hi, x, core).
Axes of the slice: x: 4, y: 4 (y_hi: 2, y_lo: 2; y = y_hi * 2 + y_lo), z: 8, core: 2. Of those that a mesh axis runs over, the one named last changes fastest.
Arguments:
- self_energy: float32 [16, 2, 8, 1024, 2048], P('tm', None, None, 'orb'), may hold values from -0.0625 to 0.0625
- history: float32 [16, 2, 1024, 1024], P('tm', None, 'orb'), may hold values from -8 to 8
- memory: int32 [1], replicated, may hold values from 3 to 8
- startup_cut: int32 [16], P('tm'), may hold values from 0 to 2048
- weight_index: int32 [16, 8], P('tm'), may hold values from 0 to 15
- weight_table: float32 [16], replicated, may hold values from 0.3 to 3
Outputs:
- collision: float32 [16, 2048, 1024], P('tm', 'orb')
All inputs are finite; a program needn't handle non-finite values.
Results may differ from a plain program's by a relative error of at most 0.0003.
Values sent between devices are 32-bit elements; how exact they have to be, the bound alone decides.
A program may use at most 128 MiB of HBM per device.

v0:
```python
import functools

import jax
import jax.numpy as jnp
from jax import lax
from jax.experimental import pallas as pl
from jax.experimental.pallas import tpu as pltpu
from jax.sharding import PartitionSpec as P

F32 = jnp.float32
BF16 = jnp.bfloat16
MESH = pl.DeviceIdType.MESH
NT = 16
LAGS = 8
CH = 8
W = 128
ZERO = 16
ORDER = (2, 1, 3, 0)
PLANS = {
    3: (
        {
            "S1": -10, "R2": -5, "R3": 0, "W": 0, "KA": 3, "KB": 4, "K0": 8, "C": 7,
            "X": 12, "F": 18,
        },
        ("F", "X", "R3", "KA", "C", "R2", "S1", "W", "K0", "KB"),
    ),
    4: (
        {
            "S1": -14, "R2": -10, "R3": -5, "R4": 0, "P1": -11, "W": 0, "KA": 2, "KB": 4,
            "K0": 6, "C": 7, "X": 14, "F": 19,
        },
        ("S1", "C", "R2", "KB", "P1", "F", "K0", "R3", "X", "KA", "R4", "W"),
    ),
    5: (
        {
            "S1": -29, "R2": -14, "R3": -9, "R4": -5, "P1": -17, "P2": -12, "W": 0, "KA": 3,
            "KB": 4, "K0": 9, "C": 7, "X": 12, "F": 20,
        },
        ("F", "S1", "P1", "X", "KA", "P2", "R3", "R4", "KB", "R2", "C", "K0", "W"),
    ),
    8: (
        {
            "S1": -21, "D7": -13, "R2": -14, "R6": -8, "R3": -10, "R4": -5, "R5": -4, "P1": -22,
            "P2": -14, "W": 0, "KA": 2, "KB": 5, "K0": 10, "C": 7, "X": 13, "F": 17,
        },
        ("R2", "W", "C", "D7", "R4", "X", "KB", "R5", "F", "R6", "S1", "R3", "P2", "P1", "KA", "K0"),
    ),
}


def halves(value):
    high = value.astype(BF16)
    return high, (value - high.astype(F32)).astype(BF16)


def kernel(
    keep, mem_ref, cut_ref, index_ref, table_ref, hist_ref, se_ref, out_ref,
    stage, rhs, own_hist, gat, via, gx, own, oth, core_in, a_in, bc_in, y_in,
    se_sem, g_send, g_recv, v_recv, k_send, k_recv, a_send, a_recv, b_send, c_send, bc_recv, y_send, y_recv,
):
    ups = min(4, keep - 1)
    downs = keep > 5
    by_via = {3: (), 4: (1,)}.get(keep, (1, 2))
    AT, PLAN = PLANS[keep]
    t = lax.axis_index("tm")
    o = lax.axis_index("orb")
    yh, x, core = o // 8, (o // 2) % 4, o % 2

    def orb_of(yh_, x_, core_):
        return yh_ * 8 + x_ * 2 + core_

    up, down = t + 1, t - 1
    partner = (t, orb_of(yh, x, 1 - core))
    right = (t, orb_of(yh, (x + 1) % 4, core))
    left = (t, orb_of(yh, (x + 3) % 4, core))
    across = (t, orb_of(1 - yh, x, core))

    for lag in range(keep):
        pltpu.make_async_copy(se_ref.at[0, :, lag], stage.at[lag], se_sem.at[lag]).start()

    barrier = pltpu.get_barrier_semaphore()
    greet = [(t <= 14, t + 1), (t >= 1, t - 1)]
    if by_via:
        greet += [(t == 7, 15), (t == 15, 7), (t == 15, 8), (t == 8, 15)]
    if downs:
        greet += [
            (t <= 7, t + 7), ((t >= 7) & (t <= 14), t - 7),
            ((t == 9) | (t == 10), 15), (t == 15, 9), (t == 15, 10),
            ((t == 1) | (t == 2), 7), (t == 7, 1), (t == 7, 2),
        ]
    count = 4
    for there, who in greet:
        count = count + there.astype(jnp.int32)

        @pl.when(there)
        def _():
            pl.semaphore_signal(barrier, inc=1, device_id=(who, o), device_id_type=MESH)

    for who in (partner, right, left, across):
        pl.semaphore_signal(barrier, inc=1, device_id=who, device_id_type=MESH)

    for c in range(CH):
        own_hist[c] = hist_ref[:, c * W:(c + 1) * W].T
    for lag in range(1, keep):

        @pl.when(t < lag)
        def _():
            gat[lag] = jnp.zeros((CH, W, W), F32)

    pl.semaphore_wait(barrier, count)

    def remote(src, dst, send, recv, who):
        return pltpu.make_async_remote_copy(
            src_ref=src, dst_ref=dst, send_sem=send, recv_sem=recv, device_id=who, device_id_type=MESH
        )

    def go(make, c):
        @pl.when(c >= 2)
        def _():
            make(c - 2).wait_send()

        make(c).start()

    def history(src, lag, c, kind, who):
        return remote(src, gat.at[lag, c], g_send.at[kind, c % 2], g_recv.at[lag, c], (who, o))

    def send_own_up(c):
        return history(own_hist.at[c], 1, c, 1, up)

    def relay(lag, c):
        if lag <= 4:
            return history(gat.at[lag - 1, c], lag, c, lag, up)
        return history(gat.at[lag + 1, c], lag, c, lag, down)

    def send_own_far(c):
        return history(own_hist.at[c], 7 - jnp.maximum(t - 8, 0), c, 7, jnp.minimum(t + 7, 15))

    def send_own_seven(c):
        return history(own_hist.at[c], 7 - t, c, 6, 7)

    def relay_via(lag, c):
        src = own_hist.at[c] if lag == 1 else gat.at[1, c]
        return remote(src, via.at[lag - 1, c], g_send.at[lag, c % 2], v_recv.at[lag - 1, c], (15, o))

    def pass_via(lag, c):
        return history(via.at[lag - 1, c], lag, c, lag, 8)

    def comes(lag):
        return lag <= ups if lag <= 4 else downs

    def relays(lag):
        if lag >= 5:
            return (t - 1 >= lag) & (t != 8)
        if lag in by_via:
            return (t <= 14) & (t + 1 >= lag) & (t != 7)
        return (t <= 14) & (t + 1 >= lag)

    def arrived(lag, c):
        remote(gat.at[lag, c], gat.at[lag, c], g_send.at[lag, 0], g_recv.at[lag, c], partner).wait_recv()

    def inside(at):
        return (at >= ZERO) & (at < ZERO + CH)

    def chunk_of(at):
        return jnp.clip(at, ZERO, ZERO + CH - 1) - ZERO

    def take_and_relay(there, lag, nxt, c):
        if comes(lag):

            @pl.when(there & (t >= lag))
            def _():
                arrived(lag, c)

        if nxt is not None and comes(nxt):

            @pl.when(there & relays(nxt))
            def _():
                go(functools.partial(relay, nxt), c)

            if nxt in by_via:

                @pl.when(there & (t == 7))
                def _():
                    go(functools.partial(relay_via, nxt), c)

    def to_partner(q, c):
        return remote(oth.at[c, q], core_in.at[c, q], k_send.at[q, c % 2], k_recv.at[(0, 1, 1, 2)[q], c], partner)

    def add_partner(start, size, c):
        part = core_in.at[c, pl.ds(start, size)]
        remote(part, part, k_send.at[start, c % 2], k_recv.at[(0, 1, 1, 2)[start], c], partner).wait_recv()
        own[c, pl.ds(start, size)] = own[c, pl.ds(start, size)] + core_in[c, pl.ds(start, size)]

    def a_copy(way, c):
        return remote(own.at[c, 0, way], a_in.at[c, way], a_send.at[way, c % 2], a_recv.at[c], (right, left)[way])

    def b_copy(way, c):
        return remote(
            own.at[c, 1 + way, 1 - way], bc_in.at[c, way], b_send.at[way, c % 2], bc_recv.at[c], (right, left)[way]
        )

    def c_copy(way, c):
        return remote(
            own.at[c, 1 + way, way], bc_in.at[c, 2 + way], c_send.at[way, c % 2], bc_recv.at[c], (right, left)[way]
        )

    def y_copy(c):
        return remote(own.at[c, 3, 1 - yh], y_in.at[c], y_send.at[c % 2], y_recv.at[c], across)

    def prepare(lag):
        pltpu.make_async_copy(se_ref.at[0, :, lag], stage.at[lag], se_sem.at[lag]).wait()
        weight = table_ref[index_ref[0, lag]]
        last = mem_ref[0] - 1
        base = pl.multiple_of(lag * W, W)
        low_base = pl.multiple_of(keep * W + lag * W, W)
        for q, d in enumerate(ORDER):
            for side in range(2):
                for yh_ in range(2):
                    col = pl.multiple_of(yh_ * 1024 + ((x + d) % 4) * 256 + (core if side == 0 else 1 - core) * W, W)
                    rows = col + lax.broadcasted_iota(jnp.int32, (64, W), 1)
                    kept = (lag < last) | ((lag == last) & (rows >= cut_ref[0]))
                    coef = jnp.where(kept, weight, F32(0.0))
                    place = pl.ds((q * 4 + side * 2 + yh_) * W, W)
                    value = jnp.concatenate(
                        [stage[lag, 0, :, pl.ds(col, W)] * coef, -(stage[lag, 1, :, pl.ds(col, W)] * coef)], axis=0
                    )
                    high, low = halves(value)
                    rhs[pl.ds(base, W), place] = high
                    rhs[pl.ds(low_base, W), place] = low

    def load_left(c):
        for lag in range(keep):
            high, low = halves(own_hist[c] if lag == 0 else gat[lag, c])
            gx[:W, lag * W:(lag + 1) * W] = high
            gx[W:, lag * W:(lag + 1) * W] = low

    def multiply(q, c):
        cols = pl.ds(q * 512, 512)
        both = jnp.dot(gx[...], rhs[:keep * W, cols], preferred_element_type=F32)
        more = jnp.dot(gx[:W], rhs[keep * W:, cols], preferred_element_type=F32)
        total = both[:W] + both[W:] + more
        for yh_ in range(2):
            own[c, q, yh_] = total[:, yh_ * W:(yh_ + 1) * W]
            oth[c, q, yh_] = total[:, (2 + yh_) * W:(3 + yh_) * W]
        go(functools.partial(to_partner, q), c)

    def run(name, at):
        there = inside(at)
        c = chunk_of(at)

        def when(cond):
            return pl.when(there & cond)

        if name == "S1":

            @when(relays(1))
            def _():
                go(send_own_up, c)

            if 1 in by_via:

                @when(t == 7)
                def _():
                    go(functools.partial(relay_via, 1), c)

        if name == "D7" and downs:

            @when(t <= 10)
            def _():
                go(send_own_far, c)

            @when((t == 1) | (t == 2))
            def _():
                go(send_own_seven, c)

        if name in ("P1", "P2") and int(name[1]) in by_via:
            lag = int(name[1])

            @when(t == 15)
            def _():
                relay_via(lag, c).wait_recv()
                go(functools.partial(pass_via, lag), c)

        if name in ("R2", "R3", "R4"):
            take_and_relay(there, int(name[1]) - 1, int(name[1]), c)
        if name in ("R5", "R6"):
            take_and_relay(there, int(name[1]) + 1, int(name[1]), c)
        if name == "W":
            take_and_relay(there, 4, None, c)
            take_and_relay(there, 5, None, c)

            @pl.when(there)
            def _():
                load_left(c)

        if name == "KA":

            @pl.when(there)
            def _():
                add_partner(0, 1, c)
                for way in range(2):
                    go(functools.partial(a_copy, way), c)

        if name == "KB":

            @pl.when(there)
            def _():
                add_partner(1, 2, c)
                for way in range(2):
                    go(functools.partial(b_copy, way), c)

        if name == "K0":

            @pl.when(there)
            def _():
                add_partner(3, 1, c)

        if name == "C":

            @pl.when(there)
            def _():
                remote(a_in.at[c], a_in.at[c], a_send.at[0, 0], a_recv.at[c], left).wait_recv()
                for way in range(2):
                    own[c, 1 + way, way] = own[c, 1 + way, way] + a_in[c, way]
                    go(functools.partial(c_copy, way), c)

        if name == "X":

            @pl.when(there)
            def _():
                remote(bc_in.at[c], bc_in.at[c], b_send.at[0, 0], bc_recv.at[c], left).wait_recv()
                own[c, 3, 0] = own[c, 3, 0] + (bc_in[c, 2] + bc_in[c, 1])
                own[c, 3, 1] = own[c, 3, 1] + (bc_in[c, 0] + bc_in[c, 3])
                go(y_copy, c)

        if name == "F":

            @pl.when(there)
            def _():
                y_copy(c).wait_recv()
                total = own[c, 3, yh] + y_in[c]
                out_ref[:, pl.ds(pl.multiple_of(c * W, W), W)] = total.T

    first = ZERO + min(AT.values()) // 4
    last = ZERO + CH + max(AT.values()) // 4

    def step(s, carry):
        for slot in range(4):
            for name in PLAN:
                if AT[name] % 4 == slot:
                    run(name, s - AT[name] // 4)

            @pl.when(inside(s))
            def _():
                multiply(slot, chunk_of(s))

            turn = s * 4 + slot
            base = max(first, ZERO - 4) * 4

            @pl.when((turn >= base) & (turn < base + keep))
            def _():
                prepare(jnp.clip(turn, base, base + keep - 1) - base)

        return carry

    lax.fori_loop(first, last + 1, step, 0)

    for c in (CH - 2, CH - 1):
        ends = [(relays(1), send_own_up)]
        for lag in range(2, keep):
            if lag != 7 and comes(lag):
                ends.append((relays(lag), functools.partial(relay, lag)))
        for lag in by_via:
            ends += [(t == 7, functools.partial(relay_via, lag)), (t == 15, functools.partial(pass_via, lag))]
        if downs:
            ends += [(t <= 10, send_own_far), ((t == 1) | (t == 2), send_own_seven)]
        for there, make in ends:

            @pl.when(there)
            def _():
                make(c).wait_send()

        for q in range(4):
            to_partner(q, c).wait_send()
        for way in range(2):
            for make in (a_copy, b_copy, c_copy):
                make(way, c).wait_send()
        y_copy(c).wait_send()


def collide(keep, memory, startup_cut, weight_index, weight_table, history, self_energy):
    smem = pl.BlockSpec(memory_space=pltpu.SMEM)
    vmem = pl.BlockSpec(memory_space=pltpu.VMEM)
    dma = pltpu.SemaphoreType.DMA
    piece = (W, W)
    return pl.pallas_call(
        functools.partial(kernel, keep),
        out_shape=jax.ShapeDtypeStruct((W, CH * W), F32),
        in_specs=[smem, smem, smem, smem, vmem, pl.BlockSpec(memory_space=pl.ANY)],
        out_specs=vmem,
        scratch_shapes=[
            pltpu.VMEM((keep, 2, 64, 2048), F32),
            pltpu.VMEM((2 * keep * W, 2048), BF16),
            pltpu.VMEM((CH, *piece), F32),
            pltpu.VMEM((keep, CH, *piece), F32),
            pltpu.VMEM((2, CH, *piece), F32),
            pltpu.VMEM((2 * W, keep * W), BF16),
            pltpu.VMEM((CH, 4, 2, *piece), F32),
            pltpu.VMEM((CH, 4, 2, *piece), F32),
            pltpu.VMEM((CH, 4, 2, *piece), F32),
            pltpu.VMEM((CH, 2, *piece), F32),
            pltpu.VMEM((CH, 4, *piece), F32),
            pltpu.VMEM((CH, *piece), F32),
            dma((keep,)),
            dma((keep, 2)), dma((keep, CH)), dma((2, CH)),
            dma((4, 2)), dma((3, CH)),
            dma((2, 2)), dma((CH,)),
            dma((2, 2)), dma((2, 2)), dma((CH,)),
            dma((2,)), dma((CH,)),
        ],
        compiler_params=pltpu.CompilerParams(
            collective_id=keep, has_side_effects=True, vmem_limit_bytes=60 * 1024 * 1024
        ),
        name=f"collision{keep}",
    )(memory, startup_cut, weight_index, weight_table, history, self_energy)


def local(self_energy, history, memory, startup_cut, weight_index, weight_table):
    keeps = tuple(PLANS)
    which = sum((memory[0] > keep).astype(jnp.int32) for keep in keeps[:-1])
    out = lax.switch(
        which,
        [functools.partial(collide, keep) for keep in keeps],
        memory, startup_cut, weight_index, weight_table, history.reshape(2 * 64, 1024), self_energy,
    )
    return out[None]


def solution(mesh):
    in_specs = (
        P("tm", None, None, "orb", None),
        P("tm", None, "orb", None),
        P(),
        P("tm"),
        P("tm", None),
        P(),
    )
    out_specs = P("tm", "orb", None)
    return jax.shard_map(local, mesh=mesh, in_specs=in_specs, out_specs=out_specs, check_vma=False)
```

profile of v0, /device:TPU:8, one launch (start us, length us, event | category | flops | bytes accessed | tf_op | source)
XLA Modules:
  0.0 85.0 jit_solution(9088152148287158128)
XLA Ops:
  0.7 83.6 %conditional.1 = (f32[1,128,1024]{2,1,0:T(8,128)S(1)}) conditional(s32[]{:T(128)} %bitcast.4, (s32[1]{0:T(128)}, s32[1]{0:T(128)}, s32[1,8]{1,0:T(1,128)}, f32[16]{0:T(128)}, f32[128,1024]{1,0:T(8,128)}, /*index=5*/f32[1,2,8,64,2048]{4,3,2,1,0:T(8,128)}) %tuple.30, (s32[1]{0:T(128)}, s32[1]{0:T(128)}, ...), branch_computations={%region_0.0_spmd, %region_1.0_spmd, %region_2.0_spmd, %region_3.0_... | conditional | bytes 8 | solution.py:431
  0.7 83.3 %collision8.1 = f32[128,1024]{1,0:T(8,128)S(1)} custom-call(s32[1]{0:T(128)} %get-tuple-element.77.mem_ref, s32[1]{0:T(128)} %get-tuple-element.78.cut_ref, s32[1,8]{1,0:T(1,128)} %get-tuple-element.79.index_ref, f32[16]{0:T(128)} %get-tuple-element.80.table_ref, f32[128,1024]{1,0:T(8,128)} %get-tuple-element.81.hist_ref, ...), custom_call_target="tpu_custom_call" | custom-call | tf_op jit(solution)/shard_map/cond/branch_3_fun/collision8/pallas_call | solution.py:396
  84.2 0.8 copy.17
where the time goes:
time: 85.4 us; the launch traced here: 85 us
  Pallas kernels  83.3 us (98%)
    pallas_call x1, Pallas kernels, collide(): pl.pallas_call(functools.partial(kernel, keep), out_shape=jax.ShapeDtypeS...  83.3 us

commit v1 on v0

--- a/solution.py
+++ b/solution.py
@@ -40,10 +40,10 @@
     ),
     8: (
         {
-            "S1": -21, "D7": -13, "R2": -14, "R6": -8, "R3": -10, "R4": -5, "R5": -4, "P1": -22,
-            "P2": -14, "W": 0, "KA": 2, "KB": 5, "K0": 10, "C": 7, "X": 13, "F": 17,
+            "S1": -20, "D7": -12, "R2": -14, "R6": -6, "R3": -10, "R4": -5, "R5": -3, "P1": -18,
+            "P2": -11, "W": 0, "KA": 2, "KB": 5, "K0": 9, "C": 6, "X": 14, "F": 18,
         },
-        ("R2", "W", "C", "D7", "R4", "X", "KB", "R5", "F", "R6", "S1", "R3", "P2", "P1", "KA", "K0"),
+        ("S1", "R4", "X", "F", "D7", "R2", "KA", "R6", "P1", "C", "KB", "R3", "K0", "P2", "R5", "W"),
     ),
 }
 

time: 85.4 us -> 81.4 us (0.953); the launches traced: 85 us -> 80 us
  Pallas kernels: 83.3 us -> 78.3 us
    pallas_call x1, Pallas kernels: 83.3 us -> 78.3 us  [collide(): pl.pallas_call(functools.partial(kernel, keep), out_shape=jax.ShapeDtypeS...]
where the time goes in v1:
time: 81.4 us; the launch traced here: 80 us
  Pallas kernels  78.3 us (96%)
    pallas_call x1, Pallas kernels, collide(): pl.pallas_call(functools.partial(kernel, keep), out_shape=jax.ShapeDtypeS...  78.3 us

profile of v1, /device:TPU:8, one launch (start us, length us, event | category | flops | bytes accessed | tf_op | source)
XLA Modules:
  0.0 80.0 jit_solution(11623652345731952928)
XLA Ops:
  0.7 78.5 %conditional.1 = (f32[1,128,1024]{2,1,0:T(8,128)S(1)}) conditional(s32[]{:T(128)} %bitcast.4, (s32[1]{0:T(128)}, s32[1]{0:T(128)}, s32[1,8]{1,0:T(1,128)}, f32[16]{0:T(128)}, f32[128,1024]{1,0:T(8,128)}, /*index=5*/f32[1,2,8,64,2048]{4,3,2,1,0:T(8,128)}) %tuple.30, (s32[1]{0:T(128)}, s32[1]{0:T(128)}, ...), branch_computations={%region_0.0_spmd, %region_1.0_spmd, %region_2.0_spmd, %region_3.0_... | conditional | bytes 8 | solution.py:431
  0.7 78.3 %collision5.1 = f32[128,1024]{1,0:T(8,128)S(1)} custom-call(s32[1]{0:T(128)} %get-tuple-element.71.mem_ref, s32[1]{0:T(128)} %get-tuple-element.72.cut_ref, s32[1,8]{1,0:T(1,128)} %get-tuple-element.73.index_ref, f32[16]{0:T(128)} %get-tuple-element.74.table_ref, f32[128,1024]{1,0:T(8,128)} %get-tuple-element.75.hist_ref, ...), custom_call_target="tpu_custom_call" | custom-call | tf_op jit(solution)/shard_map/cond/branch_2_fun/collision5/pallas_call | solution.py:396
  79.2 0.8 copy.17
